TPU v7x, 32 devices: a whole 2x2x4 slice. The times are simulated.
32 devices in a mesh: dp: 2 (over x), expert: 16 (over z, y, core).
Axes of the slice: x: 2, y: 2, z: 4, core: 2. Of those that a mesh axis runs over, the one named last changes fastest.
Arguments:
- tokens: bfloat16 [4096, 1024], P(('dp', 'expert')), may hold values from -6 to 6
- cotangent: bfloat16 [4096, 1024], P(('dp', 'expert')), may hold values from -6 to 6
- expert_ids: int32 [4096, 6], P(('dp', 'expert')), may hold values from 0 to 15, all different within a row; in each aligned block of 128 rows (0 to 127, 128 to 255, ...) at most 60 rows name the same one
- gate_weights: float32 [4096, 6], P(('dp', 'expert')), may hold values from 0.05 to 0.3
- partner: int32 [16], replicated, may hold values from 0 to 15, as said below
- weights: bfloat16 [16, 1024, 3, 384], P('expert', 'dp'), may hold values from -0.3125 to 0.3125
- first_moment: bfloat16 [16, 1024, 3, 384], P('expert', 'dp'), may hold values from -6 to 6
- second_moment: bfloat16 [16, 1024, 3, 384], P('expert', 'dp'), may hold values from 0.099609375 to 4
Outputs:
- mixed: bfloat16 [4096, 1024], P(('dp', 'expert'))
- token_grad: bfloat16 [4096, 1024], P(('dp', 'expert'))
- new_weights: bfloat16 [16, 1024, 3, 384], P('expert', 'dp')
- new_first: bfloat16 [16, 1024, 3, 384], P('expert', 'dp')
- new_second: bfloat16 [16, 1024, 3, 384], P('expert', 'dp')
Inputs may be any that keep to these rules, and one draw needn't show every extreme that they name: `expert_ids`: each row names 6 different experts. Among the 128 tokens of one device (aligned blocks of rows), no expert is named by more than 60 tokens, and in every draw some block names some expert exactly 60 times. partner[partner[h]] = h and partner[h] != h for every h.
All inputs are finite; a program needn't handle non-finite values.
Results may differ from a plain program's by a relative error of at most 0.024.
Values may be sent and summed in bfloat16 or wider, within the bound.
A program may use at most 64 MiB of HBM per device.

v0:
```python
import jax
import jax.numpy as jnp
from jax import lax
from jax.sharding import PartitionSpec as P

beta_one = 0.9
beta_two = 0.95
learn_rate = 0.01
decay_rate = 0.1
eps_adam = 1e-08
step_count = 100


def send_rows(parts):
    return (lax.all_to_all(parts[0], "expert", split_axis=0, concat_axis=0, tiled=True),)


def send_back(parts):
    return (lax.all_to_all(parts[0], "expert", split_axis=0, concat_axis=0, tiled=True),)


def shards_by_slot(
    tokens, cotangent, expert_ids, gate_weights, partner, weights, first_moment, second_moment
):
    experts_here = lax.axis_size("expert")
    tok_dev, model_width = tokens.shape
    top_count = expert_ids.shape[1]
    hidden_width = weights.shape[3]
    capacity = min(tok_dev, max(2, 5 * tok_dev * top_count // (4 * experts_here)))
    item_total = tok_dev * top_count
    slot_total = experts_here * capacity
    flat_ids = expert_ids.reshape(item_total)
    onehot = (flat_ids[:, None] == jnp.arange(experts_here, dtype=jnp.int32)[None, :]).astype(
        jnp.int32
    )
    before = jnp.cumsum(onehot, axis=0) - onehot
    slot_of = jnp.sum(before * onehot, axis=1)
    position = flat_ids * capacity + slot_of
    source = (
        jnp.full((slot_total,), item_total, jnp.int32)
        .at[position]
        .set(jnp.arange(item_total, dtype=jnp.int32))
    )
    token_of = source // top_count
    zero_row = jnp.zeros((1, model_width), jnp.bfloat16)
    x_send = jnp.concatenate([tokens, zero_row], axis=0)[token_of].reshape(
        experts_here, capacity, model_width
    )
    gate_flat = gate_weights.reshape(item_total)
    gate_pad = jnp.concatenate([gate_flat, jnp.zeros((1,), jnp.float32)])
    cot_rows = jnp.concatenate([cotangent, zero_row], axis=0)[token_of].astype(jnp.float32)
    dy_send = (
        (gate_pad[source][:, None] * cot_rows)
        .astype(jnp.bfloat16)
        .reshape(experts_here, capacity, model_width)
    )
    gathered = lax.all_gather(weights, "dp", axis=1, tiled=True)[0]
    gate_up = gathered[:, 0:2, :].reshape(model_width, 2 * hidden_width)
    down_proj = gathered[:, 2, :]
    block_shape = (experts_here, capacity, model_width)
    (x_recv,) = send_rows((x_send,))
    forward_x_rows = x_recv.reshape(slot_total, model_width)
    both_proj = jnp.dot(forward_x_rows, gate_up, preferred_element_type=jnp.float32)
    pre_act = both_proj[:, :hidden_width]
    lin_act = both_proj[:, hidden_width:]
    sigmoid_pre = jax.nn.sigmoid(pre_act)
    silu_pre = pre_act * sigmoid_pre
    forward_hidden = (silu_pre * lin_act).astype(jnp.bfloat16)
    out_rows = jnp.dot(forward_hidden, down_proj.T, preferred_element_type=jnp.float32).astype(
        jnp.bfloat16
    )
    x_rows, saved, hidden, out_rows = (
        forward_x_rows,
        (pre_act, lin_act, sigmoid_pre, silu_pre),
        forward_hidden,
        out_rows,
    )
    (out_back,) = send_back((out_rows.reshape(block_shape),))
    (dy_recv,) = send_rows((dy_send,))
    pre_act, lin_act, sigmoid_pre, silu_pre = saved
    backward_dy_rows = dy_recv.reshape(slot_total, model_width)
    hidden_grad = jnp.dot(backward_dy_rows, down_proj, preferred_element_type=jnp.float32)
    pre_grad = (hidden_grad * lin_act * sigmoid_pre * (1.0 + pre_act * (1.0 - sigmoid_pre))).astype(
        jnp.bfloat16
    )
    lin_grad = (hidden_grad * silu_pre).astype(jnp.bfloat16)
    backward_both_grad = jnp.concatenate([pre_grad, lin_grad], axis=1)
    item_grad = jnp.dot(backward_both_grad, gate_up.T, preferred_element_type=jnp.float32).astype(
        jnp.bfloat16
    )
    dy_rows, both_grad, item_grad = (backward_dy_rows, backward_both_grad, item_grad)
    (grad_back,) = send_back((item_grad.reshape(block_shape),))
    out_items = (
        out_back.reshape(slot_total, model_width)[position].astype(jnp.float32) * gate_flat[:, None]
    )
    mixed = jnp.sum(out_items.reshape(tok_dev, top_count, model_width), axis=1).astype(jnp.bfloat16)
    grad_items = grad_back.reshape(slot_total, model_width)[position].astype(jnp.float32)
    token_grad = jnp.sum(grad_items.reshape(tok_dev, top_count, model_width), axis=1).astype(
        jnp.bfloat16
    )
    count = lax.axis_size("dp") * weights.shape[1]
    proj_grad = jnp.dot(x_rows.T, both_grad, preferred_element_type=jnp.float32)
    down_grad = jnp.dot(dy_rows.T, hidden, preferred_element_type=jnp.float32)
    grad_sum = lax.psum_scatter(
        jnp.concatenate(
            [proj_grad.reshape(count, 2, hidden_width), down_grad.reshape(count, 1, hidden_width)],
            axis=1,
        ).astype(jnp.bfloat16),
        "dp",
        scatter_dimension=0,
        tiled=True,
    ).astype(jnp.float32)
    w_old = weights[0].astype(jnp.float32)
    m_old = first_moment[0].astype(jnp.float32)
    v_old = second_moment[0].astype(jnp.float32)
    m_new = beta_one * m_old + (1.0 - beta_one) * grad_sum
    v_new = beta_two * v_old + (1.0 - beta_two) * grad_sum * grad_sum
    m_hat = m_new / (1.0 - beta_one**step_count)
    v_hat = v_new / (1.0 - beta_two**step_count)
    w_new = w_old - learn_rate * (m_hat / (jnp.sqrt(v_hat) + eps_adam) + decay_rate * w_old)
    pieces = (
        w_new.astype(jnp.bfloat16).reshape(experts_here, -1),
        m_new.astype(jnp.bfloat16).reshape(experts_here, -1),
        v_new.astype(jnp.bfloat16).reshape(experts_here, -1),
    )
    spread = (
        lax.all_to_all(pieces[0], "expert", split_axis=0, concat_axis=0, tiled=True),
        lax.all_to_all(pieces[1], "expert", split_axis=0, concat_axis=0, tiled=True),
        lax.all_to_all(pieces[2], "expert", split_axis=0, concat_axis=0, tiled=True),
    )
    ordered = (spread[0][partner], spread[1][partner], spread[2][partner])
    homed = (
        lax.all_to_all(ordered[0], "expert", split_axis=0, concat_axis=0, tiled=True),
        lax.all_to_all(ordered[1], "expert", split_axis=0, concat_axis=0, tiled=True),
        lax.all_to_all(ordered[2], "expert", split_axis=0, concat_axis=0, tiled=True),
    )
    new_weights = homed[0].reshape(weights.shape)
    new_first = homed[1].reshape(weights.shape)
    new_second = homed[2].reshape(weights.shape)
    return (mixed, token_grad, new_weights, new_first, new_second)


def adam(w_old, m_old, v_old, grad_sum):
    m_new = beta_one * m_old + (1.0 - beta_one) * grad_sum
    v_new = beta_two * v_old + (1.0 - beta_two) * grad_sum * grad_sum
    m_hat = m_new / (1.0 - beta_one**step_count)
    v_hat = v_new / (1.0 - beta_two**step_count)
    w_new = w_old - learn_rate * (m_hat / (jnp.sqrt(v_hat) + eps_adam) + decay_rate * w_old)
    return (w_new, m_new, v_new)


def shards_dense(
    tokens, cotangent, expert_ids, gate_weights, partner, weights, first_moment, second_moment
):
    experts_here = lax.axis_size("expert")
    me = lax.axis_index("expert")
    tok_dev, model_width = tokens.shape
    own_rows, hidden_width = (weights.shape[1], weights.shape[3])
    width = 3 * hidden_width
    f32, bf16 = (jnp.float32, jnp.bfloat16)
    hits = expert_ids[:, :, None] == jnp.arange(experts_here, dtype=jnp.int32)[None, None, :]
    gate_table = jnp.sum(jnp.where(hits, gate_weights[:, :, None], 0.0), axis=1).T
    w_flat = weights[0].reshape(own_rows, width)
    gathered = lax.all_gather(w_flat, "dp", axis=0, tiled=True)
    x_rows = lax.all_gather(tokens, "expert", axis=0, tiled=True)
    cot_rows = lax.all_gather(cotangent, "expert", axis=0, tiled=True)
    gate_all = lax.all_gather(gate_table, "expert", axis=0)
    gate = lax.dynamic_index_in_dim(gate_all, me, 1, keepdims=False)
    gate = gate.reshape(experts_here * tok_dev, 1)
    gate_up = gathered[:, : 2 * hidden_width]
    down_proj = gathered[:, 2 * hidden_width :]
    both_proj = jnp.dot(x_rows, gate_up, preferred_element_type=f32)
    pre_act = both_proj[:, :hidden_width]
    lin_act = both_proj[:, hidden_width:]
    sigmoid_pre = jax.nn.sigmoid(pre_act)
    silu_pre = pre_act * sigmoid_pre
    hidden = (silu_pre * lin_act).astype(bf16)
    out_rows = jnp.dot(hidden, down_proj.T, preferred_element_type=f32)
    mixed = lax.psum_scatter(
        (gate * out_rows).astype(bf16), "expert", scatter_dimension=0, tiled=True
    )
    dy_rows = (gate * cot_rows.astype(f32)).astype(bf16)
    hidden_grad = jnp.dot(dy_rows, down_proj, preferred_element_type=f32)
    pre_grad = hidden_grad * lin_act * sigmoid_pre * (1.0 + pre_act * (1.0 - sigmoid_pre))
    lin_grad = hidden_grad * silu_pre
    both_grad = jnp.concatenate([pre_grad.astype(bf16), lin_grad.astype(bf16)], axis=1)
    proj_grad = jnp.dot(x_rows.T, both_grad, preferred_element_type=f32)
    down_grad = jnp.dot(dy_rows.T, hidden, preferred_element_type=f32)
    partial = jnp.concatenate([proj_grad.astype(bf16), down_grad.astype(bf16)], axis=1)
    grad_sum = lax.psum_scatter(partial, "dp", scatter_dimension=0, tiled=True).astype(f32)
    item_grad = jnp.dot(both_grad, gate_up.T, preferred_element_type=f32).astype(bf16)
    token_grad = lax.psum_scatter(item_grad, "expert", scatter_dimension=0, tiled=True)
    m_flat = first_moment[0].reshape(own_rows, width)
    v_flat = second_moment[0].reshape(own_rows, width)
    new_state = adam(w_flat.astype(f32), m_flat.astype(f32), v_flat.astype(f32), grad_sum)
    share = own_rows // experts_here
    outs = []
    for part in new_state:
        pieces = part.astype(bf16).reshape(experts_here, share, width)
        spread = lax.all_to_all(pieces, "expert", split_axis=0, concat_axis=0, tiled=True)
        homed = lax.all_to_all(spread[partner], "expert", split_axis=0, concat_axis=0, tiled=True)
        outs.append(homed.reshape(weights.shape))
    return (mixed, token_grad, *outs)


def shards(*args):
    replica_rows = lax.axis_size("expert") * args[0].shape[0]
    if replica_rows <= 4096 and args[5].shape[1] % (16 * lax.axis_size("expert")) == 0:
        return shards_dense(*args)
    return shards_by_slot(*args)


def solution(mesh):
    in_specs = (
        P(("dp", "expert"), None),
        P(("dp", "expert"), None),
        P(("dp", "expert"), None),
        P(("dp", "expert"), None),
        P(),
        P("expert", "dp", None, None),
        P("expert", "dp", None, None),
        P("expert", "dp", None, None),
    )
    out_specs = (
        P(("dp", "expert"), None),
        P(("dp", "expert"), None),
        P("expert", "dp", None, None),
        P("expert", "dp", None, None),
        P("expert", "dp", None, None),
    )
    return jax.shard_map(shards, mesh=mesh, in_specs=in_specs, out_specs=out_specs, check_vma=False)
```

profile of v0, /device:TPU:15, one launch (start us, length us, event | category | flops | bytes accessed | tf_op | source)
XLA Modules:
  0.0 465.4 jit_solution(3843170583067933573)
XLA Ops:
  7.2 0.0 copy-start.5
  7.2 0.0 copy-start.4
  7.2 0.0 all-gather.7.cloned.1.call-start
  7.2 2.4 copy.29
  9.6 0.0 all-gather.7.cloned.1.call-update
  9.6 0.0 all-gather.5.cloned.1.call-start
  9.7 0.7 all-gather.5.cloned.1.call-update
  10.4 0.0 all-gather.9.cloned.1.call-start
  10.4 0.7 all-gather.9.cloned.1.call-update
  11.1 0.0 reduce-scatter.8.cloned.1.call-start
  11.2 0.0 copy-done.5
  11.2 0.0 copy-done.4
  11.2 16.0 %all-gather = f32[256,128]{1,0:T(8,128)S(1)} all-gather(f32[16,128]{1,0:T(8,128)S(1)} %bitcast.29), channel_id=2, replica_groups=mesh['dp'=2,'expert'=16] {'expert'}, dimensions={0}, use_global_device_ids=true | all-gather | bytes 139264 | tf_op jit(solution)/shard_map/all_gather | solution.py:167
  27.2 19.2 %all-gather.7.cloned.1.call-done = bf16[1024,1152]{0,1:T(8,128)(2,1)} async-done(((bf16[512,1152]{0,1:T(8,128)(2,1)}), bf16[1024,1152]{0,1:T(8,128)(2,1)}) %all-gather.7.cloned.1.call-update) | async-done | bytes 2359312 | tf_op jit(solution)/shard_map/all_gather | solution.py:164
  46.4 53.2 %all-gather.5.cloned.1.call-done = bf16[2048,1024]{1,0:T(8,128)(2,1)} async-done(((bf16[128,1024]{1,0:T(8,128)(2,1)}), bf16[2048,1024]{1,0:T(8,128)(2,1)}) %all-gather.5.cloned.1.call-update) | async-done | bytes 4194320 | tf_op jit(solution)/shard_map/all_gather | solution.py:165
  99.6 8.7 %fusion.14 = f32[2048,768]{0,1:T(8,128)} fusion(bf16[2048,1024]{1,0:T(8,128)(2,1)} %all-gather.5.cloned.1.call-done, bf16[1024,1152]{0,1:T(8,128)(2,1)} %all-gather.7.cloned.1.call-done), kind=kOutput, calls=%fused_computation.32 | convolution fusion | flops 3221225472 | bytes 12058624 | tf_op jit(solution)/shard_map/dot_general | solution.py:172
  108.4 42.5 %all-gather.9.cloned.1.call-done = bf16[2048,1024]{1,0:T(8,128)(2,1)} async-done(((bf16[128,1024]{1,0:T(8,128)(2,1)}), bf16[2048,1024]{1,0:T(8,128)(2,1)}) %all-gather.9.cloned.1.call-update) | async-done | bytes 4194320 | tf_op jit(solution)/shard_map/all_gather | solution.py:166
  150.9 7.5 %multiply_convert_fusion.3 = (bf16[2048,384]{0,1:T(8,128)(2,1)S(1)}, bf16[2048,384]{0,1:T(8,128)(2,1)S(1)}, bf16[2048,384]{0,1:T(8,128)(2,1)S(1)}) fusion(f32[2048,768]{0,1:T(8,128)} %fusion.14, bf16[1024,1152]{0,1:T(8,128)(2,1)} %all-gather.7.cloned.1.call-done, bf16[2048,1024]{1,0:T(8,128)(2,1)} %all-gather.9.cloned.1.call-done, f32[2048]{0:T(1024)S(1)} %bitcast.30), kind=kOutput, calls=%fused_computation.9 | convolution fusion | flops 1628700672 | bytes 15998976 | tf_op jit(solution)/shard_map/dot_general | solution.py:183
  158.3 0.0 copy-start.9
  158.4 1.9 fusion.12
  160.3 0.4 copy-done.11
  160.7 1.5 copy-done.6
  162.2 3.4 fusion.10
  165.7 1.6 pad_maximum_fusion.1
  167.3 0.0 reduce-scatter.8.cloned.1.call-update
  167.4 1.2 copy-done.3
  168.6 0.2 convert_multiply_fusion.3
  168.8 2.3 copy.30
  171.1 1.5 convert_multiply_fusion.2
  172.6 0.0 copy-start
  172.6 2.0 copy.31
  174.6 25.7 %reduce-scatter.8.cloned.1.call-done = bf16[512,1152]{0,1:T(8,128)(2,1)} async-done(((bf16[1024,1152]{0,1:T(8,128)(2,1)}), bf16[512,1152]{0,1:T(8,128)(2,1)}) %reduce-scatter.8.cloned.1.call-update) | async-done | bytes 1179664 | tf_op jit(solution)/shard_map/reduce_scatter | solution.py:190
  200.3 0.0 copy-done
  200.3 5.8 %fusion.16 = (bf16[512,1152]{0,1:T(8,128)(2,1)S(1)}, bf16[512,1152]{0,1:T(8,128)(2,1)}, bf16[512,1152]{0,1:T(8,128)(2,1)S(1)}) fusion(bf16[512,1152]{0,1:T(8,128)(2,1)} %reduce-scatter.8.cloned.1.call-done, f32[1,512,3,384]{1,3,2,0:T(8,128)} %copy.31, f32[1,512,3,384]{1,3,2,0:T(8,128)} %copy.30, bf16[1,512,3,384]{1,3,2,0:T(8,128)(2,1)S(1)} %copy-done), kind=kLoop, calls=%fused_computation.34 | loop fusion | flops 10616832 | bytes 10616832 | tf_op jit(solution)/shard_map/convert_element_type | solution.py:199
  206.1 2.4 copy.32
  208.5 6.4 %all-to-all-start = ((bf16[16,32,1152]{2,1,0:T(8,128)(2,1)}), bf16[16,32,1152]{2,1,0:T(8,128)(2,1)S(1)}, u32[]{:S(2)}, u32[]{:S(2)}) async-start(bf16[16,32,1152]{2,1,0:T(8,128)(2,1)} %bitcast.7), calls=%async_computation.3 | async-start | bytes 2359296 | tf_op jit(solution)/shard_map/all_to_all | solution.py:200
  214.9 0.0 reduce-scatter.6.cloned.1.call-start
  214.9 7.8 %convolution_convert_fusion = bf16[2048,1024]{1,0:T(8,128)(2,1)} fusion(bf16[2048,384]{0,1:T(8,128)(2,1)} %copy-done.11, bf16[2048,384]{0,1:T(8,128)(2,1)} %copy-done.10, bf16[1024,1152]{0,1:T(8,128)(2,1)} %all-gather.7.cloned.1.call-done), kind=kOutput, calls=%fused_computation.5 | convolution fusion | flops 3229614080 | bytes 8912896 | tf_op jit(solution)/shard_map/dot_general | solution.py:191
  222.7 0.0 reduce-scatter.6.cloned.1.call-update
  222.7 1.4 copy.33
  224.1 18.5 %all-to-all-done = bf16[16,32,1152]{2,1,0:T(8,128)(2,1)S(1)} async-done(((bf16[16,32,1152]{2,1,0:T(8,128)(2,1)}), bf16[16,32,1152]{2,1,0:T(8,128)(2,1)S(1)}, u32[]{:S(2)}, u32[]{:S(2)}) %all-to-all-start) | async-done | bytes 1179680 | tf_op jit(solution)/shard_map/all_to_all | solution.py:200
  242.6 4.9 %all-to-all-start.2 = ((bf16[16,32,1152]{2,1,0:T(8,128)(2,1)}), bf16[16,32,1152]{2,1,0:T(8,128)(2,1)S(1)}, u32[]{:S(2)}, u32[]{:S(2)}) async-start(bf16[16,32,1152]{2,1,0:T(8,128)(2,1)} %bitcast.8), calls=%async_computation.5 | async-start | bytes 2359296 | tf_op jit(solution)/shard_map/all_to_all | solution.py:200
  247.5 1.4 copy.34
  248.9 43.1 %all-to-all-done.2 = bf16[16,32,1152]{2,1,0:T(8,128)(2,1)S(1)} async-done(((bf16[16,32,1152]{2,1,0:T(8,128)(2,1)}), bf16[16,32,1152]{2,1,0:T(8,128)(2,1)S(1)}, u32[]{:S(2)}, u32[]{:S(2)}) %all-to-all-start.2) | async-done | bytes 1179680 | tf_op jit(solution)/shard_map/all_to_all | solution.py:200
  292.1 4.9 %all-to-all-start.4 = ((bf16[16,32,1152]{2,1,0:T(8,128)(2,1)}), bf16[16,32,1152]{2,1,0:T(8,128)(2,1)S(1)}, u32[]{:S(2)}, u32[]{:S(2)}) async-start(bf16[16,32,1152]{2,1,0:T(8,128)(2,1)} %bitcast.27), calls=%async_computation.7 | async-start | bytes 2359296 | tf_op jit(solution)/shard_map/all_to_all | solution.py:200
  297.0 1.7 gather_fusion
  298.6 33.8 %all-to-all-done.4 = bf16[16,32,1152]{2,1,0:T(8,128)(2,1)S(1)} async-done(((bf16[16,32,1152]{2,1,0:T(8,128)(2,1)}), bf16[16,32,1152]{2,1,0:T(8,128)(2,1)S(1)}, u32[]{:S(2)}, u32[]{:S(2)}) %all-to-all-start.4) | async-done | bytes 1179680 | tf_op jit(solution)/shard_map/all_to_all | solution.py:200
  332.4 5.1 %all-to-all-start.1 = ((bf16[16,32,1152]{2,1,0:T(8,128)(2,1)}), bf16[16,32,1152]{2,1,0:T(8,128)(2,1)S(1)}, u32[]{:S(2)}, u32[]{:S(2)}) async-start(bf16[16,32,1152]{2,1,0:T(8,128)(2,1)} %gather_fusion), calls=%async_computation.4 | async-start | bytes 2359296 | tf_op jit(solution)/shard_map/all_to_all | solution.py:201
  337.5 0.0 reduce-scatter.4.cloned.1.call-start
  337.5 6.0 %multiply_convert_fusion.1 = bf16[2048,1024]{1,0:T(8,128)(2,1)} fusion(bf16[2048,384]{0,1:T(8,128)(2,1)} %copy-done.9, f32[2048]{0:T(1024)S(1)} %bitcast.32, bf16[1024,1152]{0,1:T(8,128)(2,1)} %all-gather.7.cloned.1.call-done), kind=kOutput, calls=%fused_computation.4 | convolution fusion | flops 1614807040 | bytes 6561792 | tf_op jit(solution)/shard_map/dot_general | solution.py:178
  343.5 0.0 reduce-scatter.4.cloned.1.call-update
  343.5 1.7 gather_fusion.1
  345.2 20.0 %all-to-all-done.1 = bf16[16,32,1152]{2,1,0:T(8,128)(2,1)S(1)} async-done(((bf16[16,32,1152]{2,1,0:T(8,128)(2,1)}), bf16[16,32,1152]{2,1,0:T(8,128)(2,1)S(1)}, u32[]{:S(2)}, u32[]{:S(2)}) %all-to-all-start.1) | async-done | bytes 1179680 | tf_op jit(solution)/shard_map/all_to_all | solution.py:201
  365.2 4.9 %all-to-all-start.3 = ((bf16[16,32,1152]{2,1,0:T(8,128)(2,1)}), bf16[16,32,1152]{2,1,0:T(8,128)(2,1)}, u32[]{:S(2)}, u32[]{:S(2)}) async-start(bf16[16,32,1152]{2,1,0:T(8,128)(2,1)} %gather_fusion.1), calls=%async_computation.6 | async-start | bytes 2359296 | tf_op jit(solution)/shard_map/all_to_all | solution.py:201
  370.1 1.7 gather_fusion.2
  371.8 43.0 %all-to-all-done.3 = bf16[16,32,1152]{2,1,0:T(8,128)(2,1)} async-done(((bf16[16,32,1152]{2,1,0:T(8,128)(2,1)}), bf16[16,32,1152]{2,1,0:T(8,128)(2,1)}, u32[]{:S(2)}, u32[]{:S(2)}) %all-to-all-start.3) | async-done | bytes 1179680 | tf_op jit(solution)/shard_map/all_to_all | solution.py:201
  414.8 5.0 %all-to-all-start.5 = ((bf16[16,32,1152]{2,1,0:T(8,128)(2,1)}), bf16[16,32,1152]{2,1,0:T(8,128)(2,1)}, u32[]{:S(2)}, u32[]{:S(2)}) async-start(bf16[16,32,1152]{2,1,0:T(8,128)(2,1)} %gather_fusion.2), calls=%async_computation.8 | async-start | bytes 2359296 | tf_op jit(solution)/shard_map/all_to_all | solution.py:201
  419.8 0.4 reshape.40
  420.2 1.2 copy.35
  421.3 2.2 reshape.42
  423.6 1.2 copy.36
  424.7 30.4 %all-to-all-done.5 = bf16[16,32,1152]{2,1,0:T(8,128)(2,1)} async-done(((bf16[16,32,1152]{2,1,0:T(8,128)(2,1)}), bf16[16,32,1152]{2,1,0:T(8,128)(2,1)}, u32[]{:S(2)}, u32[]{:S(2)}) %all-to-all-start.5) | async-done | bytes 1179680 | tf_op jit(solution)/shard_map/all_to_all | solution.py:201
  455.1 2.2 reshape.44
  457.4 1.2 copy.37
  (20 shorter events, 0.1 us)
Async XLA Ops:
  7.2 4.0 copy-start.5
  7.2 4.0 copy-start.4
  7.2 39.2 %all-gather.7.cloned.1.call-start = ((), (), s32[]{:S(2)}) async-start(), calls=%async_computation.10 | async-start | bytes 3538944 | tf_op jit(solution)/shard_map/all_gather | solution.py:164
  9.6 90.0 %all-gather.5.cloned.1.call-start = ((), (), s32[]{:S(2)}) async-start(), calls=%async_computation.9 | async-start | bytes 4456448 | tf_op jit(solution)/shard_map/all_gather | solution.py:165
  10.4 140.5 %all-gather.9.cloned.1.call-start = ((), (), s32[]{:S(2)}) async-start(), calls=%async_computation.12 | async-start | bytes 4456448 | tf_op jit(solution)/shard_map/all_gather | solution.py:166
  11.1 189.2 %reduce-scatter.8.cloned.1.call-start = ((), (), s32[]{:S(2)}) async-start(), calls=%async_computation.14 | async-start | bytes 3538944 | tf_op jit(solution)/shard_map/reduce_scatter | solution.py:190
  150.9 7.5 %copy-start.7 = (bf16[2048,1024]{1,0:T(8,128)(2,1)S(1)}, bf16[2048,1024]{1,0:T(8,128)(2,1)}, u32[]{:S(2)}) copy-start(bf16[2048,1024]{1,0:T(8,128)(2,1)} %all-gather.9.cloned.1.call-done) | copy-start | bytes 12582916
  158.3 2.0 copy-start.9
  158.3 2.0 copy-start.10
  158.4 2.4 copy-start.11
  158.4 3.9 copy-start.6
  167.3 1.3 copy-start.3
  172.6 27.7 %copy-start = (bf16[1,512,3,384]{1,3,2,0:T(8,128)(2,1)S(1)}, bf16[1,512,3,384]{1,3,2,0:T(8,128)(2,1)}, u32[]{:S(2)}) copy-start(bf16[1,512,3,384]{1,3,2,0:T(8,128)(2,1)} %copy.29) | copy-start | bytes 3538948
  208.5 34.1 %all-to-all-start = ((bf16[16,32,1152]{2,1,0:T(8,128)(2,1)}), bf16[16,32,1152]{2,1,0:T(8,128)(2,1)S(1)}, u32[]{:S(2)}, u32[]{:S(2)}) async-start(bf16[16,32,1152]{2,1,0:T(8,128)(2,1)} %bitcast.7), calls=%async_computation.3 | async-start | bytes 2359296 | tf_op jit(solution)/shard_map/all_to_all | solution.py:200
  214.9 243.7 %reduce-scatter.6.cloned.1.call-start = ((), (), s32[]{:S(2)}) async-start(), calls=%async_computation.13 | async-start | bytes 4456448 | tf_op jit(solution)/shard_map/reduce_scatter | solution.py:192
  242.6 49.4 %all-to-all-start.2 = ((bf16[16,32,1152]{2,1,0:T(8,128)(2,1)}), bf16[16,32,1152]{2,1,0:T(8,128)(2,1)S(1)}, u32[]{:S(2)}, u32[]{:S(2)}) async-start(bf16[16,32,1152]{2,1,0:T(8,128)(2,1)} %bitcast.8), calls=%async_computation.5 | async-start | bytes 2359296 | tf_op jit(solution)/shard_map/all_to_all | solution.py:200
  247.5 49.4 %copy-start.8 = (s32[16]{0:T(128)S(1)}, s32[16]{0:T(128)}, u32[]{:S(2)}) copy-start(s32[16]{0:T(128)} %param.12) | copy-start | bytes 196
  292.1 40.4 %all-to-all-start.4 = ((bf16[16,32,1152]{2,1,0:T(8,128)(2,1)}), bf16[16,32,1152]{2,1,0:T(8,128)(2,1)S(1)}, u32[]{:S(2)}, u32[]{:S(2)}) async-start(bf16[16,32,1152]{2,1,0:T(8,128)(2,1)} %bitcast.27), calls=%async_computation.7 | async-start | bytes 2359296 | tf_op jit(solution)/shard_map/all_to_all | solution.py:200
  332.4 32.8 %all-to-all-start.1 = ((bf16[16,32,1152]{2,1,0:T(8,128)(2,1)}), bf16[16,32,1152]{2,1,0:T(8,128)(2,1)S(1)}, u32[]{:S(2)}, u32[]{:S(2)}) async-start(bf16[16,32,1152]{2,1,0:T(8,128)(2,1)} %gather_fusion), calls=%async_computation.4 | async-start | bytes 2359296 | tf_op jit(solution)/shard_map/all_to_all | solution.py:201
  337.5 121.1 %reduce-scatter.4.cloned.1.call-start = ((), (), s32[]{:S(2)}) async-start(), calls=%async_computation.11 | async-start | bytes 4456448 | tf_op jit(solution)/shard_map/reduce_scatter | solution.py:179
  365.2 6.6 %copy-start.1 = (bf16[16,32,1152]{2,1,0:T(8,128)(2,1)}, bf16[16,32,1152]{2,1,0:T(8,128)(2,1)S(1)}, u32[]{:S(2)}) copy-start(bf16[16,32,1152]{2,1,0:T(8,128)(2,1)S(1)} %all-to-all-done.1) | copy-start | bytes 3538948
  365.2 49.5 %all-to-all-start.3 = ((bf16[16,32,1152]{2,1,0:T(8,128)(2,1)}), bf16[16,32,1152]{2,1,0:T(8,128)(2,1)}, u32[]{:S(2)}, u32[]{:S(2)}) async-start(bf16[16,32,1152]{2,1,0:T(8,128)(2,1)} %gather_fusion.1), calls=%async_computation.6 | async-start | bytes 2359296 | tf_op jit(solution)/shard_map/all_to_all | solution.py:201
  414.8 5.0 %copy-start.2 = (bf16[16,32,1152]{2,1,0:T(8,128)(2,1)S(1)}, bf16[16,32,1152]{2,1,0:T(8,128)(2,1)}, u32[]{:S(2)}) copy-start(bf16[16,32,1152]{2,1,0:T(8,128)(2,1)} %copy-done.1) | copy-start | bytes 3538948
  414.8 40.4 %all-to-all-start.5 = ((bf16[16,32,1152]{2,1,0:T(8,128)(2,1)}), bf16[16,32,1152]{2,1,0:T(8,128)(2,1)}, u32[]{:S(2)}, u32[]{:S(2)}) async-start(bf16[16,32,1152]{2,1,0:T(8,128)(2,1)} %gather_fusion.2), calls=%async_computation.8 | async-start | bytes 2359296 | tf_op jit(solution)/shard_map/all_to_all | solution.py:201
Sparse Core Ops, SparseCore 0:
  10.1 36.2 all-gather.6
  48.6 50.9 all-gather.4
  101.8 49.0 all-gather.8
  167.5 32.7 reduce-scatter.7
  222.9 95.5 reduce-scatter.5
  343.7 96.6 reduce-scatter.3
where the time goes:
time: 466 us; the launch traced here: 465 us
  waiting for transfers between devices  331 us (71%)
  matrix products  35.4 us (8%)
  starting transfers between devices  31.2 us (7%)
  local copies, waits for them, and re-layouts  28.5 us (6%)
  blocking collectives  16 us (3%)
  between operations  14.3 us (3%)
  other arithmetic  9.17 us (2%)
    all_to_all x3, waiting for transfers between devices, shards_dense(): lax.all_to_all(pieces, 'expert', split_axis=0, concat_axis=0, tiled=True)  95.4 us
    all_to_all x3, waiting for transfers between devices, shards_dense(): lax.all_to_all(spread[partner], 'expert', split_axis=0, concat_axis=0, ti...  93.4 us
    all_gather x1, waiting for transfers between devices, shards_dense(): x_rows = lax.all_gather(tokens, 'expert', axis=0, tiled=True)  53.2 us
    all_gather x1, waiting for transfers between devices, shards_dense(): cot_rows = lax.all_gather(cotangent, 'expert', axis=0, tiled=True)  42.5 us
    reduce_scatter x1, waiting for transfers between devices, shards_dense(): lax.psum_scatter(partial, 'dp', scatter_dimension=0, tiled=True).astype(f32)  25.7 us
    all_gather x1, waiting for transfers between devices, shards_dense(): gathered = lax.all_gather(w_flat, 'dp', axis=0, tiled=True)  19.2 us
    all_to_all x3, starting transfers between devices, shards_dense(): lax.all_to_all(pieces, 'expert', split_axis=0, concat_axis=0, tiled=True)  16.1 us
    all_gather x1, blocking collectives, shards_dense(): gate_all = lax.all_gather(gate_table, 'expert', axis=0)  16 us
  transfers between devices with their start and end apart: 12, of which 10 were waited for; matrix products, arithmetic and copies ran while one was open for 10% of the time, Pallas kernels for 0%

commit v1 on v0

--- a/solution.py
+++ b/solution.py
@@ -197,7 +197,19 @@
     outs = []
     for part in new_state:
         pieces = part.astype(bf16).reshape(experts_here, share, width)
-        spread = lax.all_to_all(pieces, "expert", split_axis=0, concat_axis=0, tiled=True)
+        ways, here = (lax.axis_size("expert"), lax.axis_index("expert"))
+        width_2 = pieces.shape[0] // ways
+        dims = list(pieces.shape)
+        dims[0] = width_2
+        height = dims[0]
+        dims[0] = height * ways
+        full = jnp.zeros(dims, pieces.dtype)
+        for mask in range(ways):
+            part_2 = lax.dynamic_slice_in_dim(pieces, (here ^ mask) * width_2, width_2, axis=0)
+            if mask:
+                part_2 = lax.ppermute(part_2, "expert", [(d, d ^ mask) for d in range(ways)])
+            full = lax.dynamic_update_slice_in_dim(full, part_2, (here ^ mask) * height, axis=0)
+        spread = full
         homed = lax.all_to_all(spread[partner], "expert", split_axis=0, concat_axis=0, tiled=True)
         outs.append(homed.reshape(weights.shape))
     return (mixed, token_grad, *outs)

time: 466 us -> 465 us (level)
  waiting for transfers between devices: 331 us -> 269 us
  starting transfers between devices: 31.2 us -> 72 us
  local copies, waits for them, and re-layouts: 28.5 us -> 47.4 us
    ppermute x0 -> x45, waiting for transfers between devices: none -> 116 us  [shards_dense(): lax.ppermute(part_2, 'expert', [(d, d ^ mask) for d in range(ways)])]
    all_to_all x3 -> x0, waiting for transfers between devices: 95.4 us -> none  [shards_dense(): lax.all_to_all(pieces, 'expert', split_axis=0, concat_axis=0, tiled=True)]
    all_to_all x3, waiting for transfers between devices: 93.4 us -> 22.8 us  [shards_dense(): lax.all_to_all(spread[partner], 'expert', split_axis=0, concat_axis=0, ti...]
    ppermute x0 -> x45, starting transfers between devices: none -> 56.1 us  [shards_dense(): lax.ppermute(part_2, 'expert', [(d, d ^ mask) for d in range(ways)])]
    all_to_all x3 -> x0, starting transfers between devices: 16.1 us -> none  [shards_dense(): lax.all_to_all(pieces, 'expert', split_axis=0, concat_axis=0, tiled=True)]
    dynamic_update_slice x0 -> x45, local copies, waits for them, and re-layouts: none -> 13.9 us  [shards_dense(): lax.dynamic_update_slice_in_dim(full, part_2, (here ^ mask) * height, axi...]
    reduce_scatter x1, waiting for transfers between devices: 25.7 us -> 14 us  [shards_dense(): lax.psum_scatter(partial, 'dp', scatter_dimension=0, tiled=True).astype(f32)]
    unnamed x28 -> x80, local copies, waits for them, and re-layouts: 9.09 us -> 11.1 us
  transfers between devices with their start and end apart: 12 -> 54, of which waited for: 10 -> 25; matrix products, arithmetic and copies ran while one was open for 10% -> 15% of each run, Pallas kernels for 0% -> 0%
where the time goes in v1:
time: 465 us; the launch traced here: 463 us
  waiting for transfers between devices  269 us (58%)
  starting transfers between devices  72 us (15%)
  local copies, waits for them, and re-layouts  47.4 us (10%)
  matrix products  34.4 us (7%)
  blocking collectives  16 us (3%)
  between operations  14.9 us (3%)
  other arithmetic  8.54 us (2%)
    ppermute x45, waiting for transfers between devices, shards_dense(): lax.ppermute(part_2, 'expert', [(d, d ^ mask) for d in range(ways)])  116 us
    ppermute x45, starting transfers between devices, shards_dense(): lax.ppermute(part_2, 'expert', [(d, d ^ mask) for d in range(ways)])  56.1 us
    all_gather x1, waiting for transfers between devices, shards_dense(): x_rows = lax.all_gather(tokens, 'expert', axis=0, tiled=True)  53.2 us
    all_gather x1, waiting for transfers between devices, shards_dense(): cot_rows = lax.all_gather(cotangent, 'expert', axis=0, tiled=True)  42.5 us
    all_to_all x3, waiting for transfers between devices, shards_dense(): lax.all_to_all(spread[partner], 'expert', split_axis=0, concat_axis=0, ti...  22.8 us
    all_gather x1, waiting for transfers between devices, shards_dense(): gathered = lax.all_gather(w_flat, 'dp', axis=0, tiled=True)  19.2 us
    all_gather x1, blocking collectives, shards_dense(): gate_all = lax.all_gather(gate_table, 'expert', axis=0)  16 us
    all_to_all x3, starting transfers between devices, shards_dense(): lax.all_to_all(spread[partner], 'expert', split_axis=0, concat_axis=0, ti...  15.4 us
  transfers between devices with their start and end apart: 54, of which 25 were waited for; matrix products, arithmetic and copies ran while one was open for 15% of the time, Pallas kernels for 0%

profile of v1, /device:TPU:15, one launch (start us, length us, event | category | flops | bytes accessed | tf_op | source)
XLA Modules:
  0.0 462.6 jit_solution(5432297077829376195)
XLA Ops:
  7.2 2.4 copy.29
  11.2 16.0 %all-gather = f32[256,128]{1,0:T(8,128)S(1)} all-gather(f32[16,128]{1,0:T(8,128)S(1)} %bitcast.31), channel_id=2, replica_groups=mesh['dp'=2,'expert'=16] {'expert'}, dimensions={0}, use_global_device_ids=true | all-gather | bytes 139264 | tf_op jit(solution)/shard_map/all_gather | solution.py:167
  27.2 19.2 %all-gather.7.cloned.1.call-done = bf16[1024,1152]{0,1:T(8,128)(2,1)} async-done(((bf16[512,1152]{0,1:T(8,128)(2,1)}), bf16[1024,1152]{0,1:T(8,128)(2,1)}) %all-gather.7.cloned.1.call-update) | async-done | bytes 2359312 | tf_op jit(solution)/shard_map/all_gather | solution.py:164
  46.4 53.2 %all-gather.5.cloned.1.call-done = bf16[2048,1024]{1,0:T(8,128)(2,1)} async-done(((bf16[128,1024]{1,0:T(8,128)(2,1)}), bf16[2048,1024]{1,0:T(8,128)(2,1)}) %all-gather.5.cloned.1.call-update) | async-done | bytes 4194320 | tf_op jit(solution)/shard_map/all_gather | solution.py:165
  99.6 8.7 %fusion.14 = f32[2048,768]{0,1:T(8,128)} fusion(bf16[2048,1024]{1,0:T(8,128)(2,1)} %all-gather.5.cloned.1.call-done, bf16[1024,1152]{0,1:T(8,128)(2,1)} %all-gather.7.cloned.1.call-done), kind=kOutput, calls=%fused_computation.32 | convolution fusion | flops 3221225472 | bytes 12058624 | tf_op jit(solution)/shard_map/dot_general | solution.py:172
  108.3 42.5 %all-gather.9.cloned.1.call-done = bf16[2048,1024]{1,0:T(8,128)(2,1)} async-done(((bf16[128,1024]{1,0:T(8,128)(2,1)}), bf16[2048,1024]{1,0:T(8,128)(2,1)}) %all-gather.9.cloned.1.call-update) | async-done | bytes 4194320 | tf_op jit(solution)/shard_map/all_gather | solution.py:166
  150.8 7.2 %multiply_convert_fusion.3 = (bf16[2048,384]{0,1:T(8,128)(2,1)S(1)}, bf16[2048,384]{0,1:T(8,128)(2,1)S(1)}, bf16[2048,384]{0,1:T(8,128)(2,1)S(1)}) fusion(f32[2048,768]{0,1:T(8,128)} %fusion.14, bf16[1024,1152]{0,1:T(8,128)(2,1)S(1)} %copy-done.33, bf16[2048,1024]{1,0:T(8,128)(2,1)} %all-gather.9.cloned.1.call-done, f32[2048]{0:T(1024)S(1)} %bitcast.32), kind=kOutput, calls=%fused_computation.9 | convolution fusion | flops 1628700672 | bytes 15998976 | tf_op jit(solution)/shard_map/dot_general | solution.py:183
  158.1 1.9 fusion.12
  160.5 1.5 copy-done.31
  162.0 3.4 fusion.10
  165.4 1.6 pad_maximum_fusion.1
  167.1 7.0 %convolution_convert_fusion = bf16[2048,1024]{1,0:T(8,128)(2,1)} fusion(bf16[2048,384]{0,1:T(8,128)(2,1)} %copy-done.37, bf16[2048,384]{0,1:T(8,128)(2,1)} %copy-done.36, bf16[1024,1152]{0,1:T(8,128)(2,1)S(1)} %copy-done.33), kind=kOutput, calls=%fused_computation.5 | convolution fusion | flops 3229614080 | bytes 8912896 | tf_op jit(solution)/shard_map/dot_general | solution.py:191
  175.6 2.0 copy.30
  177.8 2.0 copy.31
  179.8 6.1 %multiply_convert_fusion.1 = bf16[2048,1024]{1,0:T(8,128)(2,1)} fusion(bf16[2048,384]{0,1:T(8,128)(2,1)} %copy-done.35, f32[2048]{0:T(1024)S(1)} %bitcast.34, bf16[1024,1152]{0,1:T(8,128)(2,1)} %all-gather.7.cloned.1.call-done), kind=kOutput, calls=%fused_computation.4 | convolution fusion | flops 1614807040 | bytes 6561792 | tf_op jit(solution)/shard_map/dot_general | solution.py:178
  186.0 14.0 %reduce-scatter.8.cloned.1.call-done = bf16[512,1152]{0,1:T(8,128)(2,1)} async-done(((bf16[1024,1152]{0,1:T(8,128)(2,1)}), bf16[512,1152]{0,1:T(8,128)(2,1)}) %reduce-scatter.8.cloned.1.call-update) | async-done | bytes 1179664 | tf_op jit(solution)/shard_map/reduce_scatter | solution.py:190
  200.0 6.5 %fusion.16 = (bf16[512,1152]{0,1:T(8,128)(2,1)}, bf16[512,1152]{0,1:T(8,128)(2,1)}, bf16[512,1152]{0,1:T(8,128)(2,1)}) fusion(bf16[512,1152]{0,1:T(8,128)(2,1)} %reduce-scatter.8.cloned.1.call-done, f32[1,512,3,384]{1,3,2,0:T(8,128)} %copy.31, f32[1,512,3,384]{1,3,2,0:T(8,128)S(1)} %copy-done.1, bf16[1,512,3,384]{1,3,2,0:T(8,128)(2,1)S(1)} %copy-done), kind=kLoop, calls=%fused_computation.34 | loop fusion | flops 10616832 | bytes 10616832 | tf_op jit(solution)/shard_map/convert_element_type | solution.py:199
  206.5 1.7 copy.34
  210.4 1.4 collective-permute-start.32
  212.0 1.6 collective-permute-start.34
  213.6 1.8 copy.33
  215.4 1.4 copy.32
  221.5 2.6 collective-permute-start.36
  225.1 2.2 collective-permute-start.37
  229.7 2.2 collective-permute-start.39
  232.8 1.5 collective-permute-start.40
  236.3 1.6 collective-permute-done.38
  237.9 11.2 %collective-permute-done.39 = bf16[1,32,1152]{2,1,0:T(8,128)(2,1)S(1)} collective-permute-done((bf16[1,32,1152]{2,1,0:T(8,128)(2,1)S(1)}, bf16[1,32,1152]{2,1,0:T(8,128)(2,1)S(1)}, u32[]{:S(2)}, u32[]{:S(2)}) %collective-permute-start.39) | collective-permute-done | bytes 73760 | tf_op jit(solution)/shard_map/ppermute | solution.py:210
  249.1 3.3 collective-permute-done.40
  253.6 4.7 %collective-permute-done.41 = bf16[1,32,1152]{2,1,0:T(8,128)(2,1)S(1)} collective-permute-done((bf16[1,32,1152]{2,1,0:T(8,128)(2,1)S(1)}, bf16[1,32,1152]{2,1,0:T(8,128)(2,1)S(1)}, u32[]{:S(2)}, u32[]{:S(2)}) %collective-permute-start.41) | collective-permute-done | bytes 73760 | tf_op jit(solution)/shard_map/ppermute | solution.py:210
  258.8 4.0 collective-permute-done.42
  263.4 4.3 collective-permute-done.43
  267.8 2.0 collective-permute-done.44
  270.4 1.7 gather_fusion.2
  272.1 6.7 %all-to-all-start.2 = ((bf16[16,32,1152]{2,1,0:T(8,128)(2,1)}), bf16[16,32,1152]{2,1,0:T(8,128)(2,1)S(1)}, u32[]{:S(2)}, u32[]{:S(2)}) async-start(bf16[16,32,1152]{2,1,0:T(8,128)(2,1)} %gather_fusion.2), calls=%async_computation.5 | async-start | bytes 2359296 | tf_op jit(solution)/shard_map/all_to_all | solution.py:213
  280.0 2.8 collective-permute-start.21
  283.8 2.1 collective-permute-start.22
  288.1 2.1 collective-permute-start.24
  291.2 16.2 %collective-permute-done.20 = bf16[1,32,1152]{2,1,0:T(8,128)(2,1)S(1)} collective-permute-done((bf16[1,32,1152]{2,1,0:T(8,128)(2,1)}, bf16[1,32,1152]{2,1,0:T(8,128)(2,1)S(1)}, u32[]{:S(2)}, u32[]{:S(2)}) %collective-permute-start.20) | collective-permute-done | bytes 73760 | tf_op jit(solution)/shard_map/ppermute | solution.py:210
  307.4 1.4 collective-permute-start.25
  309.3 2.7 collective-permute-start.26
  312.0 7.6 %collective-permute-done.22 = bf16[1,32,1152]{2,1,0:T(8,128)(2,1)S(1)} collective-permute-done((bf16[1,32,1152]{2,1,0:T(8,128)(2,1)}, bf16[1,32,1152]{2,1,0:T(8,128)(2,1)S(1)}, u32[]{:S(2)}, u32[]{:S(2)}) %collective-permute-start.22) | collective-permute-done | bytes 73760 | tf_op jit(solution)/shard_map/ppermute | solution.py:210
  319.6 2.2 collective-permute-start.27
  323.2 2.0 collective-permute-start.29
  325.6 5.9 %collective-permute-done.26 = bf16[1,32,1152]{2,1,0:T(8,128)(2,1)S(1)} collective-permute-done((bf16[1,32,1152]{2,1,0:T(8,128)(2,1)}, bf16[1,32,1152]{2,1,0:T(8,128)(2,1)S(1)}, u32[]{:S(2)}, u32[]{:S(2)}) %collective-permute-start.26) | collective-permute-done | bytes 73760 | tf_op jit(solution)/shard_map/ppermute | solution.py:210
  332.0 3.0 collective-permute-done.27
  335.4 3.4 collective-permute-done.28
  338.8 5.3 %collective-permute-done.29 = bf16[1,32,1152]{2,1,0:T(8,128)(2,1)S(1)} collective-permute-done((bf16[1,32,1152]{2,1,0:T(8,128)(2,1)S(1)}, bf16[1,32,1152]{2,1,0:T(8,128)(2,1)S(1)}, u32[]{:S(2)}, u32[]{:S(2)}) %collective-permute-start.29) | collective-permute-done | bytes 73760 | tf_op jit(solution)/shard_map/ppermute | solution.py:210
  344.1 2.3 collective-permute-start.5
  347.2 1.3 collective-permute-start.7
  348.5 1.3 collective-permute-start.8
  350.4 1.7 gather_fusion.1
  353.4 5.8 %collective-permute-start.10 = (bf16[1,32,1152]{2,1,0:T(8,128)(2,1)}, bf16[1,32,1152]{2,1,0:T(8,128)(2,1)S(1)}, u32[]{:S(2)}, u32[]{:S(2)}) collective-permute-start(bf16[1,32,1152]{2,1,0:T(8,128)(2,1)} %get-tuple-element.57), channel_id=1, source_target_pairs={{0,11},{1,10},{2,9},{3,8},{4,15},{5,14},{6,13},{7,12},{8,3},{9,2},... | collective-permute-start | bytes 221192 | tf_op jit(solution)/shard_map/ppermute | solution.py:210
  360.2 4.3 all-to-all-start.1
  371.2 4.9 %collective-permute-start.14 = (bf16[1,32,1152]{2,1,0:T(8,128)(2,1)S(1)}, bf16[1,32,1152]{2,1,0:T(8,128)(2,1)S(1)}, u32[]{:S(2)}, u32[]{:S(2)}) collective-permute-start(bf16[1,32,1152]{2,1,0:T(8,128)(2,1)S(1)} %copy-done.8), channel_id=1, source_target_pairs={{0,15},{1,14},{2,13},{3,12},{4,11},{5,10},{6,9},{7,8},{8,7},{9,6},... | collective-permute-start | bytes 221192 | tf_op jit(solution)/shard_map/ppermute | solution.py:210
  377.0 35.8 %collective-permute-done.11 = bf16[1,32,1152]{2,1,0:T(8,128)(2,1)S(1)} collective-permute-done((bf16[1,32,1152]{2,1,0:T(8,128)(2,1)S(1)}, bf16[1,32,1152]{2,1,0:T(8,128)(2,1)S(1)}, u32[]{:S(2)}, u32[]{:S(2)}) %collective-permute-start.11) | collective-permute-done | bytes 73760 | tf_op jit(solution)/shard_map/ppermute | solution.py:210
  412.8 1.7 collective-permute-done.12
  414.6 2.3 collective-permute-done.13
  416.9 1.6 collective-permute-done.14
  418.5 1.7 gather_fusion
  420.1 4.4 all-to-all-start
  426.1 2.2 reshape.42
  429.6 22.8 %all-to-all-done = bf16[16,32,1152]{2,1,0:T(8,128)(2,1)} async-done(((bf16[16,32,1152]{2,1,0:T(8,128)(2,1)}), bf16[16,32,1152]{2,1,0:T(8,128)(2,1)}, u32[]{:S(2)}, u32[]{:S(2)}) %all-to-all-start) | async-done | bytes 1179680 | tf_op jit(solution)/shard_map/all_to_all | solution.py:213
  452.4 2.2 reshape.40
  (207 shorter events, 43.4 us)
Async XLA Ops:
  7.2 39.2 %all-gather.7.cloned.1.call-start = ((), (), s32[]{:S(2)}) async-start(), calls=%async_computation.7 | async-start | bytes 3538944 | tf_op jit(solution)/shard_map/all_gather | solution.py:164
  9.6 90.0 %all-gather.5.cloned.1.call-start = ((), (), s32[]{:S(2)}) async-start(), calls=%async_computation.6 | async-start | bytes 4456448 | tf_op jit(solution)/shard_map/all_gather | solution.py:165
  10.4 140.5 %all-gather.9.cloned.1.call-start = ((), (), s32[]{:S(2)}) async-start(), calls=%async_computation.9 | async-start | bytes 4456448 | tf_op jit(solution)/shard_map/all_gather | solution.py:166
  11.1 188.9 %reduce-scatter.8.cloned.1.call-start = ((), (), s32[]{:S(2)}) async-start(), calls=%async_computation.11 | async-start | bytes 3538944 | tf_op jit(solution)/shard_map/reduce_scatter | solution.py:190
  46.4 104.4 %copy-start.33 = (bf16[1024,1152]{0,1:T(8,128)(2,1)S(1)}, bf16[1024,1152]{0,1:T(8,128)(2,1)}, u32[]{:S(2)}) copy-start(bf16[1024,1152]{0,1:T(8,128)(2,1)} %all-gather.7.cloned.1.call-done) | copy-start | bytes 7077892
  167.1 288.7 %reduce-scatter.6.cloned.1.call-start = ((), (), s32[]{:S(2)}) async-start(), calls=%async_computation.10 | async-start | bytes 4456448 | tf_op jit(solution)/shard_map/reduce_scatter | solution.py:192
  174.1 281.7 %reduce-scatter.4.cloned.1.call-start = ((), (), s32[]{:S(2)}) async-start(), calls=%async_computation.8 | async-start | bytes 4456448 | tf_op jit(solution)/shard_map/reduce_scatter | solution.py:179
  209.4 11.0 %collective-permute-start.30 = (bf16[1,32,1152]{2,1,0:T(8,128)(2,1)}, bf16[1,32,1152]{2,1,0:T(8,128)(2,1)}, u32[]{:S(2)}, u32[]{:S(2)}) collective-permute-start(bf16[1,32,1152]{2,1,0:T(8,128)(2,1)} %get-tuple-element.35), channel_id=1, source_target_pairs={{0,1},{1,0},{2,3},{3,2},{4,5},{5,4},{6,7},{7,6},{8,9},{9,8},{10,11... | collective-permute-start | bytes 221192 | tf_op jit(solution)/shard_map/ppermute | solution.py:210
  210.1 11.4 %collective-permute-start.31 = (bf16[1,32,1152]{2,1,0:T(8,128)(2,1)}, bf16[1,32,1152]{2,1,0:T(8,128)(2,1)}, u32[]{:S(2)}, u32[]{:S(2)}) collective-permute-start(bf16[1,32,1152]{2,1,0:T(8,128)(2,1)} %get-tuple-element.34), channel_id=1, source_target_pairs={{0,2},{1,3},{2,0},{3,1},{4,6},{5,7},{6,4},{7,5},{8,10},{9,11},{10,... | collective-permute-start | bytes 221192 | tf_op jit(solution)/shard_map/ppermute | solution.py:210
  210.4 14.7 %collective-permute-start.32 = (bf16[1,32,1152]{2,1,0:T(8,128)(2,1)}, bf16[1,32,1152]{2,1,0:T(8,128)(2,1)}, u32[]{:S(2)}, u32[]{:S(2)}) collective-permute-start(bf16[1,32,1152]{2,1,0:T(8,128)(2,1)} %get-tuple-element.33), channel_id=1, source_target_pairs={{0,3},{1,2},{2,1},{3,0},{4,7},{5,6},{6,5},{7,4},{8,11},{9,10},{10,... | collective-permute-start | bytes 221192 | tf_op jit(solution)/shard_map/ppermute | solution.py:210
  211.8 16.4 %collective-permute-start.33 = (bf16[1,32,1152]{2,1,0:T(8,128)(2,1)}, bf16[1,32,1152]{2,1,0:T(8,128)(2,1)}, u32[]{:S(2)}, u32[]{:S(2)}) collective-permute-start(bf16[1,32,1152]{2,1,0:T(8,128)(2,1)} %get-tuple-element.32), channel_id=1, source_target_pairs={{0,4},{1,5},{2,6},{3,7},{4,0},{5,1},{6,2},{7,3},{8,12},{9,13},{10,... | collective-permute-start | bytes 221192 | tf_op jit(solution)/shard_map/ppermute | solution.py:210
  212.0 17.7 %collective-permute-start.34 = (bf16[1,32,1152]{2,1,0:T(8,128)(2,1)}, bf16[1,32,1152]{2,1,0:T(8,128)(2,1)}, u32[]{:S(2)}, u32[]{:S(2)}) collective-permute-start(bf16[1,32,1152]{2,1,0:T(8,128)(2,1)} %get-tuple-element.31), channel_id=1, source_target_pairs={{0,5},{1,4},{2,7},{3,6},{4,1},{5,0},{6,3},{7,2},{8,13},{9,12},{10,... | collective-permute-start | bytes 221192 | tf_op jit(solution)/shard_map/ppermute | solution.py:210
  220.4 28.7 %copy-start.19 = (bf16[1,32,1152]{2,1,0:T(8,128)(2,1)S(1)}, bf16[1,32,1152]{2,1,0:T(8,128)(2,1)}, u32[]{:S(2)}) copy-start(bf16[1,32,1152]{2,1,0:T(8,128)(2,1)} %get-tuple-element.21) | copy-start | bytes 221188
  220.5 12.3 %collective-permute-start.35 = (bf16[1,32,1152]{2,1,0:T(8,128)(2,1)S(1)}, bf16[1,32,1152]{2,1,0:T(8,128)(2,1)S(1)}, u32[]{:S(2)}, u32[]{:S(2)}) collective-permute-start(bf16[1,32,1152]{2,1,0:T(8,128)(2,1)S(1)} %copy-done.28), channel_id=1, source_target_pairs={{0,6},{1,7},{2,4},{3,5},{4,2},{5,3},{6,0},{7,1},{8,14},{9,15},{10,... | collective-permute-start | bytes 221192 | tf_op jit(solution)/shard_map/ppermute | solution.py:210
  221.5 12.8 %collective-permute-start.36 = (bf16[1,32,1152]{2,1,0:T(8,128)(2,1)S(1)}, bf16[1,32,1152]{2,1,0:T(8,128)(2,1)S(1)}, u32[]{:S(2)}, u32[]{:S(2)}) collective-permute-start(bf16[1,32,1152]{2,1,0:T(8,128)(2,1)S(1)} %copy-done.27), channel_id=1, source_target_pairs={{0,7},{1,6},{2,5},{3,4},{4,3},{5,2},{6,1},{7,0},{8,15},{9,14},{10,... | collective-permute-start | bytes 221192 | tf_op jit(solution)/shard_map/ppermute | solution.py:210
  225.1 10.5 %collective-permute-start.37 = (bf16[1,32,1152]{2,1,0:T(8,128)(2,1)S(1)}, bf16[1,32,1152]{2,1,0:T(8,128)(2,1)S(1)}, u32[]{:S(2)}, u32[]{:S(2)}) collective-permute-start(bf16[1,32,1152]{2,1,0:T(8,128)(2,1)S(1)} %copy-done.26), channel_id=1, source_target_pairs={{0,8},{1,9},{2,10},{3,11},{4,12},{5,13},{6,14},{7,15},{8,0},{9,1},... | collective-permute-start | bytes 221192 | tf_op jit(solution)/shard_map/ppermute | solution.py:210
  228.2 9.7 %collective-permute-start.38 = (bf16[1,32,1152]{2,1,0:T(8,128)(2,1)S(1)}, bf16[1,32,1152]{2,1,0:T(8,128)(2,1)S(1)}, u32[]{:S(2)}, u32[]{:S(2)}) collective-permute-start(bf16[1,32,1152]{2,1,0:T(8,128)(2,1)S(1)} %copy-done.25), channel_id=1, source_target_pairs={{0,9},{1,8},{2,11},{3,10},{4,13},{5,12},{6,15},{7,14},{8,1},{9,0},... | collective-permute-start | bytes 221192 | tf_op jit(solution)/shard_map/ppermute | solution.py:210
  229.7 19.4 %collective-permute-start.39 = (bf16[1,32,1152]{2,1,0:T(8,128)(2,1)S(1)}, bf16[1,32,1152]{2,1,0:T(8,128)(2,1)S(1)}, u32[]{:S(2)}, u32[]{:S(2)}) collective-permute-start(bf16[1,32,1152]{2,1,0:T(8,128)(2,1)S(1)} %copy-done.24), channel_id=1, source_target_pairs={{0,10},{1,11},{2,8},{3,9},{4,14},{5,15},{6,12},{7,13},{8,2},{9,3},... | collective-permute-start | bytes 221192 | tf_op jit(solution)/shard_map/ppermute | solution.py:210
  232.8 19.7 %collective-permute-start.40 = (bf16[1,32,1152]{2,1,0:T(8,128)(2,1)S(1)}, bf16[1,32,1152]{2,1,0:T(8,128)(2,1)S(1)}, u32[]{:S(2)}, u32[]{:S(2)}) collective-permute-start(bf16[1,32,1152]{2,1,0:T(8,128)(2,1)S(1)} %copy-done.23), channel_id=1, source_target_pairs={{0,11},{1,10},{2,9},{3,8},{4,15},{5,14},{6,13},{7,12},{8,3},{9,2},... | collective-permute-start | bytes 221192 | tf_op jit(solution)/shard_map/ppermute | solution.py:210
  234.3 24.0 %collective-permute-start.41 = (bf16[1,32,1152]{2,1,0:T(8,128)(2,1)S(1)}, bf16[1,32,1152]{2,1,0:T(8,128)(2,1)S(1)}, u32[]{:S(2)}, u32[]{:S(2)}) collective-permute-start(bf16[1,32,1152]{2,1,0:T(8,128)(2,1)S(1)} %copy-done.22), channel_id=1, source_target_pairs={{0,12},{1,13},{2,14},{3,15},{4,8},{5,9},{6,10},{7,11},{8,4},{9,5},... | collective-permute-start | bytes 221192 | tf_op jit(solution)/shard_map/ppermute | solution.py:210
  235.6 27.3 %collective-permute-start.42 = (bf16[1,32,1152]{2,1,0:T(8,128)(2,1)S(1)}, bf16[1,32,1152]{2,1,0:T(8,128)(2,1)S(1)}, u32[]{:S(2)}, u32[]{:S(2)}) collective-permute-start(bf16[1,32,1152]{2,1,0:T(8,128)(2,1)S(1)} %copy-done.21), channel_id=1, source_target_pairs={{0,13},{1,12},{2,15},{3,14},{4,9},{5,8},{6,11},{7,10},{8,5},{9,4},... | collective-permute-start | bytes 221192 | tf_op jit(solution)/shard_map/ppermute | solution.py:210
  237.9 29.8 %collective-permute-start.43 = (bf16[1,32,1152]{2,1,0:T(8,128)(2,1)S(1)}, bf16[1,32,1152]{2,1,0:T(8,128)(2,1)S(1)}, u32[]{:S(2)}, u32[]{:S(2)}) collective-permute-start(bf16[1,32,1152]{2,1,0:T(8,128)(2,1)S(1)} %copy-done.20), channel_id=1, source_target_pairs={{0,14},{1,15},{2,12},{3,13},{4,10},{5,11},{6,8},{7,9},{8,6},{9,7},... | collective-permute-start | bytes 221192 | tf_op jit(solution)/shard_map/ppermute | solution.py:210
  249.1 20.7 %collective-permute-start.44 = (bf16[1,32,1152]{2,1,0:T(8,128)(2,1)S(1)}, bf16[1,32,1152]{2,1,0:T(8,128)(2,1)S(1)}, u32[]{:S(2)}, u32[]{:S(2)}) collective-permute-start(bf16[1,32,1152]{2,1,0:T(8,128)(2,1)S(1)} %copy-done.19), channel_id=1, source_target_pairs={{0,15},{1,14},{2,13},{3,12},{4,11},{5,10},{6,9},{7,8},{8,7},{9,6},... | collective-permute-start | bytes 221192 | tf_op jit(solution)/shard_map/ppermute | solution.py:210
  252.5 26.5 %collective-permute-start.15 = (bf16[1,32,1152]{2,1,0:T(8,128)(2,1)}, bf16[1,32,1152]{2,1,0:T(8,128)(2,1)}, u32[]{:S(2)}, u32[]{:S(2)}) collective-permute-start(bf16[1,32,1152]{2,1,0:T(8,128)(2,1)} %get-tuple-element.51), channel_id=1, source_target_pairs={{0,1},{1,0},{2,3},{3,2},{4,5},{5,4},{6,7},{7,6},{8,9},{9,8},{10,11... | collective-permute-start | bytes 221192 | tf_op jit(solution)/shard_map/ppermute | solution.py:210
  258.3 21.8 %collective-permute-start.16 = (bf16[1,32,1152]{2,1,0:T(8,128)(2,1)}, bf16[1,32,1152]{2,1,0:T(8,128)(2,1)}, u32[]{:S(2)}, u32[]{:S(2)}) collective-permute-start(bf16[1,32,1152]{2,1,0:T(8,128)(2,1)} %get-tuple-element.50), channel_id=1, source_target_pairs={{0,2},{1,3},{2,0},{3,1},{4,6},{5,7},{6,4},{7,5},{8,10},{9,11},{10,... | collective-permute-start | bytes 221192 | tf_op jit(solution)/shard_map/ppermute | solution.py:210
  262.8 21.0 %collective-permute-start.17 = (bf16[1,32,1152]{2,1,0:T(8,128)(2,1)}, bf16[1,32,1152]{2,1,0:T(8,128)(2,1)}, u32[]{:S(2)}, u32[]{:S(2)}) collective-permute-start(bf16[1,32,1152]{2,1,0:T(8,128)(2,1)} %get-tuple-element.49), channel_id=1, source_target_pairs={{0,3},{1,2},{2,1},{3,0},{4,7},{5,6},{6,5},{7,4},{8,11},{9,10},{10,... | collective-permute-start | bytes 221192 | tf_op jit(solution)/shard_map/ppermute | solution.py:210
  267.7 19.1 %collective-permute-start.18 = (bf16[1,32,1152]{2,1,0:T(8,128)(2,1)}, bf16[1,32,1152]{2,1,0:T(8,128)(2,1)}, u32[]{:S(2)}, u32[]{:S(2)}) collective-permute-start(bf16[1,32,1152]{2,1,0:T(8,128)(2,1)} %get-tuple-element.48), channel_id=1, source_target_pairs={{0,4},{1,5},{2,6},{3,7},{4,0},{5,1},{6,2},{7,3},{8,12},{9,13},{10,... | collective-permute-start | bytes 221192 | tf_op jit(solution)/shard_map/ppermute | solution.py:210
  269.8 18.4 %collective-permute-start.19 = (bf16[1,32,1152]{2,1,0:T(8,128)(2,1)}, bf16[1,32,1152]{2,1,0:T(8,128)(2,1)}, u32[]{:S(2)}, u32[]{:S(2)}) collective-permute-start(bf16[1,32,1152]{2,1,0:T(8,128)(2,1)} %get-tuple-element.47), channel_id=1, source_target_pairs={{0,5},{1,4},{2,7},{3,6},{4,1},{5,0},{6,3},{7,2},{8,13},{9,12},{10,... | collective-permute-start | bytes 221192 | tf_op jit(solution)/shard_map/ppermute | solution.py:210
  272.1 87.0 %all-to-all-start.2 = ((bf16[16,32,1152]{2,1,0:T(8,128)(2,1)}), bf16[16,32,1152]{2,1,0:T(8,128)(2,1)S(1)}, u32[]{:S(2)}, u32[]{:S(2)}) async-start(bf16[16,32,1152]{2,1,0:T(8,128)(2,1)} %gather_fusion.2), calls=%async_computation.5 | async-start | bytes 2359296 | tf_op jit(solution)/shard_map/all_to_all | solution.py:213
  278.9 43.0 %copy-start.18 = (bf16[1,32,1152]{2,1,0:T(8,128)(2,1)S(1)}, bf16[1,32,1152]{2,1,0:T(8,128)(2,1)}, u32[]{:S(2)}) copy-start(bf16[1,32,1152]{2,1,0:T(8,128)(2,1)} %get-tuple-element.38) | copy-start | bytes 221188
  278.9 44.3 %copy-start.17 = (bf16[1,32,1152]{2,1,0:T(8,128)(2,1)S(1)}, bf16[1,32,1152]{2,1,0:T(8,128)(2,1)}, u32[]{:S(2)}) copy-start(bf16[1,32,1152]{2,1,0:T(8,128)(2,1)} %get-tuple-element.37) | copy-start | bytes 221188
  278.9 46.4 %copy-start.16 = (bf16[1,32,1152]{2,1,0:T(8,128)(2,1)S(1)}, bf16[1,32,1152]{2,1,0:T(8,128)(2,1)}, u32[]{:S(2)}) copy-start(bf16[1,32,1152]{2,1,0:T(8,128)(2,1)} %get-tuple-element.67) | copy-start | bytes 221188
  278.9 52.6 %copy-start.15 = (bf16[1,32,1152]{2,1,0:T(8,128)(2,1)S(1)}, bf16[1,32,1152]{2,1,0:T(8,128)(2,1)}, u32[]{:S(2)}) copy-start(bf16[1,32,1152]{2,1,0:T(8,128)(2,1)} %get-tuple-element.66) | copy-start | bytes 221188
  278.9 56.0 %copy-start.14 = (bf16[1,32,1152]{2,1,0:T(8,128)(2,1)S(1)}, bf16[1,32,1152]{2,1,0:T(8,128)(2,1)}, u32[]{:S(2)}) copy-start(bf16[1,32,1152]{2,1,0:T(8,128)(2,1)} %get-tuple-element.65) | copy-start | bytes 221188
  278.9 59.9 %copy-start.13 = (bf16[1,32,1152]{2,1,0:T(8,128)(2,1)S(1)}, bf16[1,32,1152]{2,1,0:T(8,128)(2,1)}, u32[]{:S(2)}) copy-start(bf16[1,32,1152]{2,1,0:T(8,128)(2,1)} %get-tuple-element.64) | copy-start | bytes 221188
  278.9 65.2 %copy-start.12 = (bf16[1,32,1152]{2,1,0:T(8,128)(2,1)S(1)}, bf16[1,32,1152]{2,1,0:T(8,128)(2,1)}, u32[]{:S(2)}) copy-start(bf16[1,32,1152]{2,1,0:T(8,128)(2,1)} %get-tuple-element.63) | copy-start | bytes 221188
  278.9 28.5 %collective-permute-start.20 = (bf16[1,32,1152]{2,1,0:T(8,128)(2,1)}, bf16[1,32,1152]{2,1,0:T(8,128)(2,1)S(1)}, u32[]{:S(2)}, u32[]{:S(2)}) collective-permute-start(bf16[1,32,1152]{2,1,0:T(8,128)(2,1)} %get-tuple-element.46), channel_id=1, source_target_pairs={{0,6},{1,7},{2,4},{3,5},{4,2},{5,3},{6,0},{7,1},{8,14},{9,15},{10,... | collective-permute-start | bytes 221192 | tf_op jit(solution)/shard_map/ppermute | solution.py:210
  280.0 29.3 %collective-permute-start.21 = (bf16[1,32,1152]{2,1,0:T(8,128)(2,1)}, bf16[1,32,1152]{2,1,0:T(8,128)(2,1)S(1)}, u32[]{:S(2)}, u32[]{:S(2)}) collective-permute-start(bf16[1,32,1152]{2,1,0:T(8,128)(2,1)} %get-tuple-element.45), channel_id=1, source_target_pairs={{0,7},{1,6},{2,5},{3,4},{4,3},{5,2},{6,1},{7,0},{8,15},{9,14},{10,... | collective-permute-start | bytes 221192 | tf_op jit(solution)/shard_map/ppermute | solution.py:210
  283.8 35.8 %collective-permute-start.22 = (bf16[1,32,1152]{2,1,0:T(8,128)(2,1)}, bf16[1,32,1152]{2,1,0:T(8,128)(2,1)S(1)}, u32[]{:S(2)}, u32[]{:S(2)}) collective-permute-start(bf16[1,32,1152]{2,1,0:T(8,128)(2,1)} %get-tuple-element.44), channel_id=1, source_target_pairs={{0,8},{1,9},{2,10},{3,11},{4,12},{5,13},{6,14},{7,15},{8,0},{9,1},... | collective-permute-start | bytes 221192 | tf_op jit(solution)/shard_map/ppermute | solution.py:210
  286.8 35.0 %collective-permute-start.23 = (bf16[1,32,1152]{2,1,0:T(8,128)(2,1)}, bf16[1,32,1152]{2,1,0:T(8,128)(2,1)S(1)}, u32[]{:S(2)}, u32[]{:S(2)}) collective-permute-start(bf16[1,32,1152]{2,1,0:T(8,128)(2,1)} %get-tuple-element.43), channel_id=1, source_target_pairs={{0,9},{1,8},{2,11},{3,10},{4,13},{5,12},{6,15},{7,14},{8,1},{9,0},... | collective-permute-start | bytes 221192 | tf_op jit(solution)/shard_map/ppermute | solution.py:210
  288.1 35.0 %collective-permute-start.24 = (bf16[1,32,1152]{2,1,0:T(8,128)(2,1)}, bf16[1,32,1152]{2,1,0:T(8,128)(2,1)S(1)}, u32[]{:S(2)}, u32[]{:S(2)}) collective-permute-start(bf16[1,32,1152]{2,1,0:T(8,128)(2,1)} %get-tuple-element.42), channel_id=1, source_target_pairs={{0,10},{1,11},{2,8},{3,9},{4,14},{5,15},{6,12},{7,13},{8,2},{9,3},... | collective-permute-start | bytes 221192 | tf_op jit(solution)/shard_map/ppermute | solution.py:210
  307.4 17.8 %collective-permute-start.25 = (bf16[1,32,1152]{2,1,0:T(8,128)(2,1)}, bf16[1,32,1152]{2,1,0:T(8,128)(2,1)S(1)}, u32[]{:S(2)}, u32[]{:S(2)}) collective-permute-start(bf16[1,32,1152]{2,1,0:T(8,128)(2,1)} %get-tuple-element.41), channel_id=1, source_target_pairs={{0,11},{1,10},{2,9},{3,8},{4,15},{5,14},{6,13},{7,12},{8,3},{9,2},... | collective-permute-start | bytes 221192 | tf_op jit(solution)/shard_map/ppermute | solution.py:210
  309.3 22.2 %collective-permute-start.26 = (bf16[1,32,1152]{2,1,0:T(8,128)(2,1)}, bf16[1,32,1152]{2,1,0:T(8,128)(2,1)S(1)}, u32[]{:S(2)}, u32[]{:S(2)}) collective-permute-start(bf16[1,32,1152]{2,1,0:T(8,128)(2,1)} %get-tuple-element.40), channel_id=1, source_target_pairs={{0,12},{1,13},{2,14},{3,15},{4,8},{5,9},{6,10},{7,11},{8,4},{9,5},... | collective-permute-start | bytes 221192 | tf_op jit(solution)/shard_map/ppermute | solution.py:210
  319.6 15.3 %collective-permute-start.27 = (bf16[1,32,1152]{2,1,0:T(8,128)(2,1)}, bf16[1,32,1152]{2,1,0:T(8,128)(2,1)S(1)}, u32[]{:S(2)}, u32[]{:S(2)}) collective-permute-start(bf16[1,32,1152]{2,1,0:T(8,128)(2,1)} %get-tuple-element.39), channel_id=1, source_target_pairs={{0,13},{1,12},{2,15},{3,14},{4,9},{5,8},{6,11},{7,10},{8,5},{9,4},... | collective-permute-start | bytes 221192 | tf_op jit(solution)/shard_map/ppermute | solution.py:210
  321.9 16.9 %collective-permute-start.28 = (bf16[1,32,1152]{2,1,0:T(8,128)(2,1)S(1)}, bf16[1,32,1152]{2,1,0:T(8,128)(2,1)S(1)}, u32[]{:S(2)}, u32[]{:S(2)}) collective-permute-start(bf16[1,32,1152]{2,1,0:T(8,128)(2,1)S(1)} %copy-done.18), channel_id=1, source_target_pairs={{0,14},{1,15},{2,12},{3,13},{4,10},{5,11},{6,8},{7,9},{8,6},{9,7},... | collective-permute-start | bytes 221192 | tf_op jit(solution)/shard_map/ppermute | solution.py:210
  323.2 20.9 %collective-permute-start.29 = (bf16[1,32,1152]{2,1,0:T(8,128)(2,1)S(1)}, bf16[1,32,1152]{2,1,0:T(8,128)(2,1)S(1)}, u32[]{:S(2)}, u32[]{:S(2)}) collective-permute-start(bf16[1,32,1152]{2,1,0:T(8,128)(2,1)S(1)} %copy-done.17), channel_id=1, source_target_pairs={{0,15},{1,14},{2,13},{3,12},{4,11},{5,10},{6,9},{7,8},{8,7},{9,6},... | collective-permute-start | bytes 221192 | tf_op jit(solution)/shard_map/ppermute | solution.py:210
  325.2 18.9 %collective-permute-start = (bf16[1,32,1152]{2,1,0:T(8,128)(2,1)S(1)}, bf16[1,32,1152]{2,1,0:T(8,128)(2,1)S(1)}, u32[]{:S(2)}, u32[]{:S(2)}) collective-permute-start(bf16[1,32,1152]{2,1,0:T(8,128)(2,1)S(1)} %copy-done.16), channel_id=1, source_target_pairs={{0,1},{1,0},{2,3},{3,2},{4,5},{5,4},{6,7},{7,6},{8,9},{9,8},{10,11... | collective-permute-start | bytes 221192 | tf_op jit(solution)/shard_map/ppermute | solution.py:210
  331.5 15.0 %collective-permute-start.1 = (bf16[1,32,1152]{2,1,0:T(8,128)(2,1)S(1)}, bf16[1,32,1152]{2,1,0:T(8,128)(2,1)S(1)}, u32[]{:S(2)}, u32[]{:S(2)}) collective-permute-start(bf16[1,32,1152]{2,1,0:T(8,128)(2,1)S(1)} %copy-done.15), channel_id=1, source_target_pairs={{0,2},{1,3},{2,0},{3,1},{4,6},{5,7},{6,4},{7,5},{8,10},{9,11},{10,... | collective-permute-start | bytes 221192 | tf_op jit(solution)/shard_map/ppermute | solution.py:210
  334.9 12.2 %collective-permute-start.2 = (bf16[1,32,1152]{2,1,0:T(8,128)(2,1)S(1)}, bf16[1,32,1152]{2,1,0:T(8,128)(2,1)S(1)}, u32[]{:S(2)}, u32[]{:S(2)}) collective-permute-start(bf16[1,32,1152]{2,1,0:T(8,128)(2,1)S(1)} %copy-done.14), channel_id=1, source_target_pairs={{0,3},{1,2},{2,1},{3,0},{4,7},{5,6},{6,5},{7,4},{8,11},{9,10},{10,... | collective-permute-start | bytes 221192 | tf_op jit(solution)/shard_map/ppermute | solution.py:210
  338.8 9.7 %collective-permute-start.3 = (bf16[1,32,1152]{2,1,0:T(8,128)(2,1)S(1)}, bf16[1,32,1152]{2,1,0:T(8,128)(2,1)S(1)}, u32[]{:S(2)}, u32[]{:S(2)}) collective-permute-start(bf16[1,32,1152]{2,1,0:T(8,128)(2,1)S(1)} %copy-done.13), channel_id=1, source_target_pairs={{0,4},{1,5},{2,6},{3,7},{4,0},{5,1},{6,2},{7,3},{8,12},{9,13},{10,... | collective-permute-start | bytes 221192 | tf_op jit(solution)/shard_map/ppermute | solution.py:210
  344.1 6.2 %collective-permute-start.4 = (bf16[1,32,1152]{2,1,0:T(8,128)(2,1)S(1)}, bf16[1,32,1152]{2,1,0:T(8,128)(2,1)S(1)}, u32[]{:S(2)}, u32[]{:S(2)}) collective-permute-start(bf16[1,32,1152]{2,1,0:T(8,128)(2,1)S(1)} %copy-done.12), channel_id=1, source_target_pairs={{0,5},{1,4},{2,7},{3,6},{4,1},{5,0},{6,3},{7,2},{8,13},{9,12},{10,... | collective-permute-start | bytes 221192 | tf_op jit(solution)/shard_map/ppermute | solution.py:210
  344.1 9.2 %collective-permute-start.5 = (bf16[1,32,1152]{2,1,0:T(8,128)(2,1)}, bf16[1,32,1152]{2,1,0:T(8,128)(2,1)}, u32[]{:S(2)}, u32[]{:S(2)}) collective-permute-start(bf16[1,32,1152]{2,1,0:T(8,128)(2,1)} %get-tuple-element.62), channel_id=1, source_target_pairs={{0,6},{1,7},{2,4},{3,5},{4,2},{5,3},{6,0},{7,1},{8,14},{9,15},{10,... | collective-permute-start | bytes 221192 | tf_op jit(solution)/shard_map/ppermute | solution.py:210
  346.5 18.9 %collective-permute-start.6 = (bf16[1,32,1152]{2,1,0:T(8,128)(2,1)}, bf16[1,32,1152]{2,1,0:T(8,128)(2,1)}, u32[]{:S(2)}, u32[]{:S(2)}) collective-permute-start(bf16[1,32,1152]{2,1,0:T(8,128)(2,1)} %get-tuple-element.61), channel_id=1, source_target_pairs={{0,7},{1,6},{2,5},{3,4},{4,3},{5,2},{6,1},{7,0},{8,15},{9,14},{10,... | collective-permute-start | bytes 221192 | tf_op jit(solution)/shard_map/ppermute | solution.py:210
  347.2 20.0 %collective-permute-start.7 = (bf16[1,32,1152]{2,1,0:T(8,128)(2,1)}, bf16[1,32,1152]{2,1,0:T(8,128)(2,1)}, u32[]{:S(2)}, u32[]{:S(2)}) collective-permute-start(bf16[1,32,1152]{2,1,0:T(8,128)(2,1)} %get-tuple-element.60), channel_id=1, source_target_pairs={{0,8},{1,9},{2,10},{3,11},{4,12},{5,13},{6,14},{7,15},{8,0},{9,1},... | collective-permute-start | bytes 221192 | tf_op jit(solution)/shard_map/ppermute | solution.py:210
  348.5 20.5 %collective-permute-start.8 = (bf16[1,32,1152]{2,1,0:T(8,128)(2,1)}, bf16[1,32,1152]{2,1,0:T(8,128)(2,1)}, u32[]{:S(2)}, u32[]{:S(2)}) collective-permute-start(bf16[1,32,1152]{2,1,0:T(8,128)(2,1)} %get-tuple-element.59), channel_id=1, source_target_pairs={{0,9},{1,8},{2,11},{3,10},{4,13},{5,12},{6,15},{7,14},{8,1},{9,0},... | collective-permute-start | bytes 221192 | tf_op jit(solution)/shard_map/ppermute | solution.py:210
  350.3 20.8 %collective-permute-start.9 = (bf16[1,32,1152]{2,1,0:T(8,128)(2,1)}, bf16[1,32,1152]{2,1,0:T(8,128)(2,1)}, u32[]{:S(2)}, u32[]{:S(2)}) collective-permute-start(bf16[1,32,1152]{2,1,0:T(8,128)(2,1)} %get-tuple-element.58), channel_id=1, source_target_pairs={{0,10},{1,11},{2,8},{3,9},{4,14},{5,15},{6,12},{7,13},{8,2},{9,3},... | collective-permute-start | bytes 221192 | tf_op jit(solution)/shard_map/ppermute | solution.py:210
  353.4 17.8 %copy-start.8 = (bf16[1,32,1152]{2,1,0:T(8,128)(2,1)S(1)}, bf16[1,32,1152]{2,1,0:T(8,128)(2,1)}, u32[]{:S(2)}) copy-start(bf16[1,32,1152]{2,1,0:T(8,128)(2,1)} %get-tuple-element.53) | copy-start | bytes 221188
  353.4 23.6 %collective-permute-start.10 = (bf16[1,32,1152]{2,1,0:T(8,128)(2,1)}, bf16[1,32,1152]{2,1,0:T(8,128)(2,1)S(1)}, u32[]{:S(2)}, u32[]{:S(2)}) collective-permute-start(bf16[1,32,1152]{2,1,0:T(8,128)(2,1)} %get-tuple-element.57), channel_id=1, source_target_pairs={{0,11},{1,10},{2,9},{3,8},{4,15},{5,14},{6,13},{7,12},{8,3},{9,2},... | collective-permute-start | bytes 221192 | tf_op jit(solution)/shard_map/ppermute | solution.py:210
  360.2 60.0 %all-to-all-start.1 = ((bf16[16,32,1152]{2,1,0:T(8,128)(2,1)}), bf16[16,32,1152]{2,1,0:T(8,128)(2,1)}, u32[]{:S(2)}, u32[]{:S(2)}) async-start(bf16[16,32,1152]{2,1,0:T(8,128)(2,1)} %gather_fusion.1), calls=%async_computation.4 | async-start | bytes 2359296 | tf_op jit(solution)/shard_map/all_to_all | solution.py:213
  365.4 47.5 %collective-permute-start.11 = (bf16[1,32,1152]{2,1,0:T(8,128)(2,1)S(1)}, bf16[1,32,1152]{2,1,0:T(8,128)(2,1)S(1)}, u32[]{:S(2)}, u32[]{:S(2)}) collective-permute-start(bf16[1,32,1152]{2,1,0:T(8,128)(2,1)S(1)} %copy-done.11), channel_id=1, source_target_pairs={{0,12},{1,13},{2,14},{3,15},{4,8},{5,9},{6,10},{7,11},{8,4},{9,5},... | collective-permute-start | bytes 221192 | tf_op jit(solution)/shard_map/ppermute | solution.py:210
  367.2 47.3 %collective-permute-start.12 = (bf16[1,32,1152]{2,1,0:T(8,128)(2,1)S(1)}, bf16[1,32,1152]{2,1,0:T(8,128)(2,1)S(1)}, u32[]{:S(2)}, u32[]{:S(2)}) collective-permute-start(bf16[1,32,1152]{2,1,0:T(8,128)(2,1)S(1)} %copy-done.10), channel_id=1, source_target_pairs={{0,13},{1,12},{2,15},{3,14},{4,9},{5,8},{6,11},{7,10},{8,5},{9,4},... | collective-permute-start | bytes 221192 | tf_op jit(solution)/shard_map/ppermute | solution.py:210
  369.0 47.9 %collective-permute-start.13 = (bf16[1,32,1152]{2,1,0:T(8,128)(2,1)S(1)}, bf16[1,32,1152]{2,1,0:T(8,128)(2,1)S(1)}, u32[]{:S(2)}, u32[]{:S(2)}) collective-permute-start(bf16[1,32,1152]{2,1,0:T(8,128)(2,1)S(1)} %copy-done.9), channel_id=1, source_target_pairs={{0,14},{1,15},{2,12},{3,13},{4,10},{5,11},{6,8},{7,9},{8,6},{9,7},... | collective-permute-start | bytes 221192 | tf_op jit(solution)/shard_map/ppermute | solution.py:210
  371.2 47.3 %collective-permute-start.14 = (bf16[1,32,1152]{2,1,0:T(8,128)(2,1)S(1)}, bf16[1,32,1152]{2,1,0:T(8,128)(2,1)S(1)}, u32[]{:S(2)}, u32[]{:S(2)}) collective-permute-start(bf16[1,32,1152]{2,1,0:T(8,128)(2,1)S(1)} %copy-done.8), channel_id=1, source_target_pairs={{0,15},{1,14},{2,13},{3,12},{4,11},{5,10},{6,9},{7,8},{8,7},{9,6},... | collective-permute-start | bytes 221192 | tf_op jit(solution)/shard_map/ppermute | solution.py:210
  420.1 32.2 %all-to-all-start = ((bf16[16,32,1152]{2,1,0:T(8,128)(2,1)}), bf16[16,32,1152]{2,1,0:T(8,128)(2,1)}, u32[]{:S(2)}, u32[]{:S(2)}) async-start(bf16[16,32,1152]{2,1,0:T(8,128)(2,1)} %gather_fusion), calls=%async_computation.3 | async-start | bytes 2359296 | tf_op jit(solution)/shard_map/all_to_all | solution.py:213
  (28 other events, 194.2 us)
Sparse Core Ops, SparseCore 0:
  10.1 36.2 all-gather.6
  48.6 50.9 all-gather.4
  101.8 49.0 all-gather.8
  167.2 32.7 reduce-scatter.7
  204.7 91.2 reduce-scatter.5
  300.3 106.0 reduce-scatter.3
